TPU v7x, 256 devices: a whole 4x4x8 slice. The times are simulated.
256 devices in a mesh: tm: 16 (over x, y), space: 16 (over z, core).
Axes of the slice: x: 4, y: 4, z: 8, core: 2. Of those that a mesh axis runs over, the one named last changes fastest.
Arguments:
- clip: bfloat16 [256, 512, 768], P('tm', 'space'), may hold values from -160 to 160
- w_spatial: bfloat16 [4, 768, 768], replicated, may hold values from -4 to 4
- w_temporal: bfloat16 [4, 768, 768], replicated, may hold values from -4 to 4
Outputs:
- result: bfloat16 [256, 512, 768], P('tm', 'space')
All inputs are finite; a program needn't handle non-finite values.
Results may differ from a plain program's by a relative error of at most 0.011.
Values may be sent and summed in bfloat16 or wider, within the bound.
A program may use at most 128 MiB of HBM per device.

v0:
```python
import math
import jax
import jax.numpy as jnp
from jax import lax
from jax.sharding import PartitionSpec as P

HEAD = 64


def rms_norm(values):
    wide = values.astype(jnp.float32)
    return (wide * lax.rsqrt(jnp.mean(wide * wide, axis=-1, keepdims=True) + 1e-06)).astype(
        jnp.bfloat16
    )


def project_three(normed, weights):
    width = normed.shape[-1]
    flat = normed.reshape(-1, width)
    stacked = jnp.einsum(
        "rd,jde->jre", flat, weights[:3], preferred_element_type=jnp.float32
    ).astype(jnp.bfloat16)
    return (
        stacked[0].reshape(normed.shape),
        stacked[1].reshape(normed.shape),
        stacked[2].reshape(normed.shape),
    )


def out_project(mixed, weight):
    width = mixed.shape[-1]
    return jnp.dot(mixed.reshape(-1, width), weight, preferred_element_type=jnp.float32).reshape(
        mixed.shape
    )


def attend_frame(parts):
    query, key, value = parts
    count, width = query.shape
    heads = width // HEAD
    qh = query.reshape(count, heads, HEAD)
    kh = key.reshape(count, heads, HEAD)
    vh = value.reshape(count, heads, HEAD)
    scores = jnp.einsum("qhd,khd->hqk", qh, kh, preferred_element_type=jnp.float32) * (
        1.0 / math.sqrt(HEAD)
    )
    largest = jnp.max(scores, axis=-1, keepdims=True)
    expo = jnp.exp(scores - largest)
    weights = (expo / jnp.sum(expo, axis=-1, keepdims=True)).astype(jnp.bfloat16)
    mixed = jnp.einsum("hqk,khd->qhd", weights, vh, preferred_element_type=jnp.float32)
    return mixed.astype(jnp.bfloat16).reshape(count, width)


def frame_block(parts):
    inner = (parts[0][0], parts[1][0], parts[2][0])
    return lax.map(attend_frame, inner)[None]


def on_device(clip, w_spatial, w_temporal):
    frames, toks, width = clip.shape
    heads = width // HEAD
    space_count = lax.axis_size("space")
    frame_shape = (space_count, frames // space_count, toks, width)
    normed = rms_norm(clip)
    sq, sk, sv = project_three(normed, w_spatial)
    smix = frame_block(
        (
            lax.all_to_all(
                sq.reshape(frame_shape), "space", split_axis=0, concat_axis=2, tiled=True
            ),
            lax.all_to_all(
                sk.reshape(frame_shape), "space", split_axis=0, concat_axis=2, tiled=True
            ),
            lax.all_to_all(
                sv.reshape(frame_shape), "space", split_axis=0, concat_axis=2, tiled=True
            ),
        )
    )
    smix = lax.all_to_all(smix, "space", split_axis=2, concat_axis=0, tiled=True).reshape(
        frames, toks, width
    )
    after_space = (clip.astype(jnp.float32) + out_project(smix, w_spatial[3])).astype(jnp.bfloat16)
    tnormed = rms_norm(after_space)
    tq, tk, tv = project_three(tnormed, w_temporal)
    first_frame = lax.axis_index("tm") * frames
    qh = tq.reshape(frames, toks, heads, HEAD)
    query_pos = first_frame + jnp.arange(frames, dtype=jnp.int32)
    running = jnp.full((frames, toks, heads), -1e30, jnp.float32)
    key_piece = lax.all_gather(tk, "tm", axis=0, tiled=True)
    value_piece = lax.all_gather(tv, "tm", axis=0, tiled=True)
    count = key_piece.shape[0]
    kh = key_piece.reshape(count, toks, heads, HEAD)
    vh = value_piece.reshape(count, toks, heads, HEAD)
    scores = jnp.einsum("fphd,gphd->fphg", qh, kh, preferred_element_type=jnp.float32) * (
        1.0 / math.sqrt(HEAD)
    )
    key_pos = jnp.arange(count, dtype=jnp.int32)
    allowed = (key_pos[None, :] <= query_pos[:, None])[:, None, None, :]
    scores = jnp.where(allowed, scores, -1e30)
    newmax = jnp.maximum(running, jnp.max(scores, axis=-1))
    expo = jnp.where(allowed, jnp.exp(scores - newmax[..., None]), 0.0)
    total = jnp.sum(expo, axis=-1)
    acc = jnp.einsum("fphg,gphd->fphd", expo, vh.astype(jnp.float32))
    running, total, acc = (newmax, total, acc)
    tmix = (acc / total[..., None]).reshape(frames, toks, width).astype(jnp.bfloat16)
    return (after_space.astype(jnp.float32) + out_project(tmix, w_temporal[3])).astype(jnp.bfloat16)


def solution(mesh):
    placed = (P("tm", "space", None), P(), P())
    return jax.shard_map(
        on_device, mesh=mesh, in_specs=placed, out_specs=P("tm", "space", None), check_vma=False
    )
```

profile of v0, /device:TPU:1, one launch (start us, length us, event | category | flops | bytes accessed | tf_op | source)
XLA Modules:
  0.0 389.2 jit_solution(14649983245477244457)
XLA Ops:
  9.2 4.0 %convert_bitcast_fusion.1 = bf16[3,512,768]{2,1,0:T(8,128)(2,1)S(1)} fusion(bf16[512,768,1]{1,0,2:T(8,128)(2,1)S(1)} %bitcast.74, bf16[4,768,768]{2,1,0:T(8,128)(2,1)} %param.4), kind=kOutput, calls=%fused_computation.30 | convolution fusion | flops 1813118976 | bytes 6684672 | tf_op jit(solution)/shard_map/rd,jde->jre/dot_general | solution.py:20
  14.3 32.7 %all_to_all.16 = bf16[16,1,32,768]{3,2,1,0:T(8,128)(2,1)} all-to-all(bf16[16,1,32,768]{3,2,1,0:T(8,128)(2,1)S(1)} %bitcast.73), channel_id=1, replica_groups=mesh['tm'=16,'space'=16] {'space'}, dimensions={0} | all-to-all | bytes 1572864 | tf_op jit(solution)/shard_map/all_to_all | solution.py:68
  47.0 25.7 %all_to_all.17 = bf16[16,1,32,768]{3,2,1,0:T(8,128)(2,1)} all-to-all(bf16[16,1,32,768]{3,2,1,0:T(8,128)(2,1)S(1)} %bitcast.72), channel_id=1, replica_groups=mesh['tm'=16,'space'=16] {'space'}, dimensions={0} | all-to-all | bytes 1572864 | tf_op jit(solution)/shard_map/all_to_all | solution.py:71
  72.7 3.5 all-to-all-start
  76.4 2.7 reshape.105
  79.1 3.8 reshape.106
  82.9 8.0 %fusion.32 = f32[12,512,512]{1,2,0:T(8,128)} fusion(bf16[512,12,64]{2,1,0:T(8,128)(2,1)} %reshape.106, bf16[512,12,64]{2,1,0:T(8,128)(2,1)S(1)} %reshape.105), kind=kOutput, calls=%fused_computation.40 | convolution fusion | flops 402653184 | bytes 14155776 | tf_op jit(solution)/shard_map/while/body/eval_jaxpr/qhd,khd->hqk/dot_general | solution.py:44
  90.9 11.1 %fusion.55 = f32[12,512]{1,0:T(8,128)S(1)} fusion(f32[12,512,512]{1,2,0:T(8,128)} %fusion.32), kind=kOutput, calls=%fused_computation.61 | output fusion | flops 12583423 | bytes 12607488 | tf_op jit(solution)/shard_map/while/body/eval_jaxpr/sub | solution.py:48
  103.4 12.5 %fusion.35 = bf16[12,64,512]{2,1,0:T(8,128)(2,1)S(1)} fusion(f32[12,512]{1,0:T(8,128)S(1)} %fusion.55, bf16[512,12,64]{2,1,0:T(8,128)(2,1)S(1)} %reshape.104, f32[12,512,512]{1,2,0:T(8,128)} %fusion.32), kind=kOutput, calls=%fused_computation.43 | convolution fusion | flops 418781696 | bytes 14180352 | tf_op jit(solution)/shard_map/while/body/eval_jaxpr/hqk,khd->qhd/dot_general | solution.py:50
  115.8 1.8 copy.40
  118.2 5.5 %reduce = bf16[512,768]{1,0:T(8,128)(2,1)S(1)} reduce(bf16[512,1,1,768]{3,2,1,0:T(2,128)(2,1)S(1)} %bitcast.68, bf16[]{:T(256)} %broadcast.73), dimensions={1,2}, to_apply=%bitcast.56.reduce_sub_computation | reduce | bytes 1572866
  123.9 29.7 %all_to_all.18 = bf16[16,2,12288]{2,1,0:T(2,128)(2,1)S(1)} all-to-all(bf16[16,2,12288]{2,1,0:T(2,128)(2,1)S(1)} %reshape.114), channel_id=1, replica_groups=mesh['tm'=16,'space'=16] {'space'}, dimensions={0} | all-to-all | bytes 1572864 | tf_op jit(solution)/shard_map/all_to_all | solution.py:79
  154.4 2.2 fusion.26
  157.5 4.0 %convert_bitcast_fusion = bf16[3,512,768]{2,1,0:T(8,128)(2,1)S(1)} fusion(bf16[512,768,1]{1,0,2:T(8,128)(2,1)S(1)} %bitcast.75, bf16[4,768,768]{2,1,0:T(8,128)(2,1)} %param.5), kind=kOutput, calls=%fused_computation.29 | convolution fusion | flops 1813118976 | bytes 6684672 | tf_op jit(solution)/shard_map/rd,jde->jre/dot_general | solution.py:20
  165.2 89.3 %all-gather.5.cloned.1.call-done = bf16[256,32,768]{2,1,0:T(8,128)(2,1)} async-done(((bf16[16,32,768]{2,1,0:T(8,128)(2,1)}), bf16[256,32,768]{2,1,0:T(8,128)(2,1)}) %all-gather.5.cloned.1.call-update) | async-done | bytes 12582928 | tf_op jit(solution)/shard_map/all_gather | solution.py:89
  254.5 16.7 %copy.42 = bf16[256,32,768]{0,2,1:T(8,128)(2,1)} copy(bf16[256,32,768]{2,1,0:T(8,128)(2,1)} %all-gather.5.cloned.1.call-done) | data formatting | bytes 25165824 | tf_op jit(solution)/shard_map/all_gather | solution.py:89
  271.1 6.0 %fusion.6 = (f32[16,32,12]{0,2,1:T(8,128)S(1)}, f32[32,12,256,16]{2,3,1,0:T(8,128)S(1)}) fusion(pred[16,256]{1,0:T(8,128)(4,1)S(1)} %iota_compare_fusion, bf16[256,32,12,64]{0,3,2,1:T(8,128)(2,1)} %bitcast.66, bf16[16,32,12,64]{3,2,1,0:T(8,128)(2,1)S(1)} %reshape_reshape_squeeze.15), kind=kOutput, calls=%fused_computation.9 | convolution fusion | flops 206039040 | bytes 19689472 | tf_op jit(solution)/shard_map/fphd,gphd->fphg/dot_general | solution.py:94
  277.2 2.7 copy-done
  279.9 2.1 fusion.7
  282.0 69.5 %all-gather.3.cloned.1.call-done = bf16[256,32,768]{2,1,0:T(8,128)(2,1)} async-done(((bf16[16,32,768]{2,1,0:T(8,128)(2,1)}), bf16[256,32,768]{2,1,0:T(8,128)(2,1)}) %all-gather.3.cloned.1.call-update) | async-done | bytes 12582928 | tf_op jit(solution)/shard_map/all_gather | solution.py:90
  351.5 16.7 %copy.41 = bf16[256,32,768]{0,2,1:T(8,128)(2,1)} copy(bf16[256,32,768]{2,1,0:T(8,128)(2,1)} %all-gather.3.cloned.1.call-done) | data formatting | bytes 25165824 | tf_op jit(solution)/shard_map/all_gather | solution.py:90
  368.3 8.3 %fusion.13 = bf16[16,32,12,64]{3,0,2,1:T(8,128)(2,1)S(1)} fusion(f32[16,32,12]{0,2,1:T(8,128)S(1)} %fusion.7, bf16[256,32,12,64]{0,3,2,1:T(8,128)(2,1)} %bitcast.67, f32[32,12,256,16]{2,3,1,0:T(8,128)} %copy-done, f32[16,32,12]{0,2,1:T(8,128)S(1)} %broadcast_maximum_fusion, pred[16,256]{1,0:T(8,128)(4,1)S(1)} %iota_compare_fusion), kind=kOutput, calls=%fused_computation.17 | convolution fusion | flops 208404480 | bytes 19714048 | tf_op jit(solution)/shard_map/fphg,gphd->fphd/dot_general | solution.py:103
  377.1 2.0 convert_element_type.65
  379.2 3.2 fusion.28
  (29 shorter events, 11.9 us)
Async XLA Ops:
  72.7 29.4 %all-to-all-start = ((bf16[16,1,32,768]{3,2,1,0:T(8,128)(2,1)}), bf16[16,1,32,768]{3,2,1,0:T(8,128)(2,1)S(1)}, u32[]{:S(2)}, u32[]{:S(2)}) async-start(bf16[16,1,32,768]{3,2,1,0:T(8,128)(2,1)} %bitcast.4), calls=%async_computation | async-start | bytes 1572864 | tf_op jit(solution)/shard_map/all_to_all | solution.py:74
  76.2 178.3 %all-gather.5.cloned.1.call-start = ((), (), s32[]{:S(2)}) async-start(), calls=%async_computation.5 | async-start | bytes 13369344 | tf_op jit(solution)/shard_map/all_gather | solution.py:89
  118.2 36.2 %copy-start.1 = (bf16[16,32,768]{2,1,0:T(8,128)(2,1)S(1)}, bf16[16,32,768]{2,1,0:T(8,128)(2,1)}, u32[]{:S(2)}) copy-start(bf16[16,32,768]{2,1,0:T(8,128)(2,1)} %param.3) | copy-start | bytes 2359300
  156.6 0.9 copy-start.2
  162.9 188.6 %all-gather.3.cloned.1.call-start = ((), (), s32[]{:S(2)}) async-start(), calls=%async_computation.4 | async-start | bytes 13369344 | tf_op jit(solution)/shard_map/all_gather | solution.py:90
  277.2 2.7 copy-start
  376.6 2.6 copy-start.3
Sparse Core Ops, SparseCore 0:
  163.0 91.4 all-gather.4
  256.9 94.5 all-gather.2
where the time goes:
time: 391 us; the launch traced here: 389 us
  waiting for transfers between devices  159 us (41%)
  blocking collectives  88 us (23%)
  local copies, waits for them, and re-layouts  54.3 us (14%)
  matrix products  48.2 us (12%)
  other arithmetic  21.7 us (6%)
  between operations  13.6 us (3%)
    all_gather x1, waiting for transfers between devices, on_device(): key_piece = lax.all_gather(tk, 'tm', axis=0, tiled=True)  89.3 us
    all_gather x1, waiting for transfers between devices, on_device(): value_piece = lax.all_gather(tv, 'tm', axis=0, tiled=True)  69.5 us
    all_to_all x1, blocking collectives, on_device(): lax.all_to_all(sq.reshape(frame_shape), 'space', split_axis=0, concat_axi...  32.7 us
    all_to_all x1, blocking collectives, on_device(): lax.all_to_all(smix, 'space', split_axis=2, concat_axis=0, tiled=True)  29.7 us
    all_to_all x1, blocking collectives, on_device(): lax.all_to_all(sk.reshape(frame_shape), 'space', split_axis=0, concat_axi...  25.7 us
    all_gather x1, local copies, waits for them, and re-layouts, on_device(): value_piece = lax.all_gather(tv, 'tm', axis=0, tiled=True)  16.7 us
    all_gather x1, local copies, waits for them, and re-layouts, on_device(): key_piece = lax.all_gather(tk, 'tm', axis=0, tiled=True)  16.7 us
    dot_general x1, matrix products, attend_frame(): jnp.einsum('hqk,khd->qhd', weights, vh, preferred_element_type=jnp.float32)  12.5 us
  transfers between devices with their start and end apart: 3, of which 2 were waited for; matrix products, arithmetic and copies ran while one was open for 13% of the time, Pallas kernels for 0%

commit v1 on v0

--- a/solution.py
+++ b/solution.py
@@ -87,7 +87,9 @@
     query_pos = first_frame + jnp.arange(frames, dtype=jnp.int32)
     running = jnp.full((frames, toks, heads), -1e30, jnp.float32)
     key_piece = lax.all_gather(tk, "tm", axis=0, tiled=True)
-    value_piece = lax.all_gather(tv, "tm", axis=0, tiled=True)
+    value_piece = jnp.concatenate(
+        lax.all_to_all(jnp.stack([tv] * lax.axis_size("tm")), "tm", 0, 0), axis=0
+    )
     count = key_piece.shape[0]
     kh = key_piece.reshape(count, toks, heads, HEAD)
     vh = value_piece.reshape(count, toks, heads, HEAD)

time: 391 us -> 510 us (1.30); the launches traced: 389 us -> 501 us
  waiting for transfers between devices: 159 us -> 229 us
  local copies, waits for them, and re-layouts: 54.3 us -> 81.5 us
  matrix products: 48.2 us -> 56.4 us
  starting transfers between devices: 3.78 us -> 10.5 us
    all_to_all x0 -> x1, waiting for transfers between devices: none -> 229 us  [on_device(): lax.all_to_all(jnp.stack([tv] * lax.axis_size('tm')), 'tm', 0, 0)]
    all_gather x1, waiting for transfers between devices: 89.3 us -> 0.01 us  [on_device(): key_piece = lax.all_gather(tk, 'tm', axis=0, tiled=True)]
    all_gather x1 -> x0, waiting for transfers between devices: 69.5 us -> none  [on_device(): value_piece = lax.all_gather(tv, 'tm', axis=0, tiled=True)]
    another operation x0 -> x2, local copies, waits for them, and re-layouts: none -> 44.4 us  [the longest x1 38.3 us: on_device(): vh = value_piece.reshape(count, toks, heads, HEAD)]
    all_gather x1 -> x0, local copies, waits for them, and re-layouts: 16.7 us -> none  [on_device(): value_piece = lax.all_gather(tv, 'tm', axis=0, tiled=True)]
    dot_general x1, matrix products: 8.34 us -> 16.6 us  [on_device(): acc = jnp.einsum('fphg,gphd->fphd', expo, vh.astype(jnp.float32))]
    all_to_all x1, blocking collectives: 25.7 us -> 32.7 us  [on_device(): lax.all_to_all(sk.reshape(frame_shape), 'space', split_axis=0, concat_axi...]
    all_to_all x1, blocking collectives: 32.7 us -> 25.7 us  [on_device(): lax.all_to_all(sq.reshape(frame_shape), 'space', split_axis=0, concat_axi...]
  transfers between devices with their start and end apart: 3 -> 3, of which waited for: 2 -> 1; matrix products, arithmetic and copies ran while one was open for 13% -> 14% of each run, Pallas kernels for 0% -> 0%
where the time goes in v1:
time: 510 us; the launch traced here: 501 us
  waiting for transfers between devices  229 us (45%)
  blocking collectives  88 us (17%)
  local copies, waits for them, and re-layouts  81.5 us (16%)
  matrix products  56.4 us (11%)
  other arithmetic  21.8 us (4%)
  between operations  13.6 us (3%)
  starting transfers between devices  10.5 us (2%)
    all_to_all x1, waiting for transfers between devices, on_device(): lax.all_to_all(jnp.stack([tv] * lax.axis_size('tm')), 'tm', 0, 0)  229 us
    another operation x1, local copies, waits for them, and re-layouts, on_device(): vh = value_piece.reshape(count, toks, heads, HEAD)  38.3 us
    all_to_all x1, blocking collectives, on_device(): lax.all_to_all(sk.reshape(frame_shape), 'space', split_axis=0, concat_axi...  32.7 us
    all_to_all x1, blocking collectives, on_device(): lax.all_to_all(smix, 'space', split_axis=2, concat_axis=0, tiled=True)  29.7 us
    all_to_all x1, blocking collectives, on_device(): lax.all_to_all(sq.reshape(frame_shape), 'space', split_axis=0, concat_axi...  25.7 us
    all_gather x1, local copies, waits for them, and re-layouts, on_device(): key_piece = lax.all_gather(tk, 'tm', axis=0, tiled=True)  16.8 us
    dot_general x1, matrix products, on_device(): acc = jnp.einsum('fphg,gphd->fphd', expo, vh.astype(jnp.float32))  16.6 us
    dot_general x1, matrix products, attend_frame(): jnp.einsum('hqk,khd->qhd', weights, vh, preferred_element_type=jnp.float32)  12.5 us
  transfers between devices with their start and end apart: 3, of which 1 were waited for; matrix products, arithmetic and copies ran while one was open for 14% of the time, Pallas kernels for 0%

profile of v1, /device:TPU:1, one launch (start us, length us, event | category | flops | bytes accessed | tf_op | source)
XLA Modules:
  0.0 500.8 jit_solution(13046796380715723492)
XLA Ops:
  9.2 4.0 convert_bitcast_fusion.1
  14.3 32.7 %all_to_all.20 = bf16[16,1,32,768]{3,2,1,0:T(8,128)(2,1)} all-to-all(bf16[16,1,32,768]{3,2,1,0:T(8,128)(2,1)S(1)} %bitcast.72), channel_id=1, replica_groups=mesh['tm'=16,'space'=16] {'space'}, dimensions={0} | all-to-all | bytes 1572864 | tf_op jit(solution)/shard_map/all_to_all | solution.py:71
  47.0 25.7 %all_to_all.42 = bf16[16,1,32,768]{3,2,1,0:T(8,128)(2,1)} all-to-all(bf16[16,1,32,768]{3,2,1,0:T(8,128)(2,1)S(1)} %bitcast.71), channel_id=1, replica_groups=mesh['tm'=16,'space'=16] {'space'}, dimensions={0} | all-to-all | bytes 1572864 | tf_op jit(solution)/shard_map/all_to_all | solution.py:68
  72.7 3.5 all-to-all-start
  76.4 2.7 reshape.104
  79.1 3.8 reshape.105
  82.9 8.0 %fusion.33 = f32[12,512,512]{1,2,0:T(8,128)} fusion(bf16[512,12,64]{2,1,0:T(8,128)(2,1)} %reshape.105, bf16[512,12,64]{2,1,0:T(8,128)(2,1)S(1)} %reshape.104), kind=kOutput, calls=%fused_computation.41 | convolution fusion | flops 402653184 | bytes 14155776 | tf_op jit(solution)/shard_map/while/body/eval_jaxpr/qhd,khd->hqk/dot_general | solution.py:44
  90.9 11.1 %fusion.58 = f32[12,512]{1,0:T(8,128)S(1)} fusion(f32[12,512,512]{1,2,0:T(8,128)} %fusion.33), kind=kOutput, calls=%fused_computation.62 | output fusion | flops 12583423 | bytes 12607488 | tf_op jit(solution)/shard_map/while/body/eval_jaxpr/sub | solution.py:48
  103.4 12.5 %fusion.36 = bf16[12,64,512]{2,1,0:T(8,128)(2,1)S(1)} fusion(f32[12,512]{1,0:T(8,128)S(1)} %fusion.58, bf16[512,12,64]{2,1,0:T(8,128)(2,1)S(1)} %reshape.103, f32[12,512,512]{1,2,0:T(8,128)} %fusion.33), kind=kOutput, calls=%fused_computation.44 | convolution fusion | flops 418781696 | bytes 14180352 | tf_op jit(solution)/shard_map/while/body/eval_jaxpr/hqk,khd->qhd/dot_general | solution.py:50
  118.2 5.5 %reduce = bf16[512,768]{1,0:T(8,128)(2,1)S(1)} reduce(bf16[512,1,1,768]{3,2,1,0:T(2,128)(2,1)S(1)} %bitcast.67, bf16[]{:T(256)} %broadcast.74), dimensions={1,2}, to_apply=%bitcast.57.reduce_sub_computation | reduce | bytes 1572866
  123.9 29.7 %all_to_all.43 = bf16[16,2,12288]{2,1,0:T(2,128)(2,1)S(1)} all-to-all(bf16[16,2,12288]{2,1,0:T(2,128)(2,1)S(1)} %reshape.112), channel_id=1, replica_groups=mesh['tm'=16,'space'=16] {'space'}, dimensions={0} | all-to-all | bytes 1572864 | tf_op jit(solution)/shard_map/all_to_all | solution.py:79
  154.4 2.2 fusion.27
  157.5 4.0 convert_bitcast_fusion
  162.6 6.2 %stack.3 = bf16[16,16,32,768]{3,2,1,0:T(8,128)(2,1)} broadcast(bf16[16,32,768]{2,1,0:T(8,128)(2,1)S(1)} %bitcast.69), dimensions={1,2,3} | broadcast | bytes 13369344 | tf_op jit(solution)/shard_map/stack | solution.py:91
  168.7 6.8 %all-to-all-start.4 = ((bf16[16,16,32,768]{3,2,1,0:T(8,128)(2,1)}), bf16[16,16,32,768]{3,2,1,0:T(8,128)(2,1)}, u32[]{:S(2)}, u32[]{:S(2)}) async-start(bf16[16,16,32,768]{3,2,1,0:T(8,128)(2,1)} %stack.3), calls=%async_computation.4 | async-start | bytes 25165824 | tf_op jit(solution)/shard_map/all_to_all | solution.py:91
  176.9 228.8 %all-to-all-done.4 = bf16[16,16,32,768]{3,2,1,0:T(8,128)(2,1)} async-done(((bf16[16,16,32,768]{3,2,1,0:T(8,128)(2,1)}), bf16[16,16,32,768]{3,2,1,0:T(8,128)(2,1)}, u32[]{:S(2)}, u32[]{:S(2)}) %all-to-all-start.4) | async-done | bytes 12582944 | tf_op jit(solution)/shard_map/all_to_all | solution.py:91
  405.7 38.3 %reshape_reshape.4 = bf16[256,32,12,64]{3,2,1,0:T(8,128)(2,1)} reshape(bf16[16,16,32,768]{3,2,1,0:T(8,128)(2,1)} %all-to-all-done.4) | data formatting | bytes 25165824 | tf_op jit(solution)/shard_map/reshape;reshape | solution.py:95
  444.0 16.8 %copy.41 = bf16[256,32,768]{0,2,1:T(8,128)(2,1)} copy(bf16[256,32,768]{2,1,0:T(8,128)(2,1)} %all-gather.2.cloned.1.call-done) | data formatting | bytes 25165824 | tf_op jit(solution)/shard_map/all_gather | solution.py:89
  460.8 6.0 %fusion.8 = (f32[16,32,12]{0,2,1:T(8,128)S(1)}, f32[32,12,256,16]{2,3,1,0:T(8,128)S(1)}) fusion(pred[16,256]{1,0:T(8,128)(4,1)S(1)} %iota_compare_fusion, bf16[256,32,12,64]{0,3,2,1:T(8,128)(2,1)} %bitcast.66, bf16[16,32,12,64]{3,2,1,0:T(8,128)(2,1)S(1)} %reshape_reshape_squeeze.15), kind=kOutput, calls=%fused_computation.11 | convolution fusion | flops 206039040 | bytes 19689472 | tf_op jit(solution)/shard_map/fphd,gphd->fphg/dot_general | solution.py:96
  466.9 2.5 copy-done
  469.5 2.1 fusion.9
  471.6 16.6 %fusion.14 = bf16[16,32,12,64]{3,0,2,1:T(8,128)(2,1)S(1)} fusion(f32[16,32,12]{0,2,1:T(8,128)S(1)} %fusion.9, f32[32,12,256,16]{2,3,1,0:T(8,128)} %copy-done, f32[16,32,12]{0,2,1:T(8,128)S(1)} %broadcast_maximum_fusion, pred[16,256]{1,0:T(8,128)(4,1)S(1)} %iota_compare_fusion, bf16[256,32,12,64]{3,2,1,0:T(8,128)(2,1)} %reshape_reshape.4), kind=kOutput, calls=%fused_computation.18 | convolution fusion | flops 208404480 | bytes 19714048 | tf_op jit(solution)/shard_map/fphg,gphd->fphd/dot_general | solution.py:105
  488.7 2.0 convert_element_type.65
  490.8 3.2 fusion.29
  (29 shorter events, 12.4 us)
Async XLA Ops:
  72.7 29.4 %all-to-all-start = ((bf16[16,1,32,768]{3,2,1,0:T(8,128)(2,1)}), bf16[16,1,32,768]{3,2,1,0:T(8,128)(2,1)S(1)}, u32[]{:S(2)}, u32[]{:S(2)}) async-start(bf16[16,1,32,768]{3,2,1,0:T(8,128)(2,1)} %bitcast.4), calls=%async_computation | async-start | bytes 1572864 | tf_op jit(solution)/shard_map/all_to_all | solution.py:74
  76.2 367.8 %all-gather.2.cloned.1.call-start = ((), (), s32[]{:S(2)}) async-start(), calls=%async_computation.5 | async-start | bytes 13369344 | tf_op jit(solution)/shard_map/all_gather | solution.py:89
  118.2 36.2 %copy-start.1 = (bf16[16,32,768]{2,1,0:T(8,128)(2,1)S(1)}, bf16[16,32,768]{2,1,0:T(8,128)(2,1)}, u32[]{:S(2)}) copy-start(bf16[16,32,768]{2,1,0:T(8,128)(2,1)} %param.3) | copy-start | bytes 2359300
  156.6 0.9 copy-start.2
  168.7 237.0 %all-to-all-start.4 = ((bf16[16,16,32,768]{3,2,1,0:T(8,128)(2,1)}), bf16[16,16,32,768]{3,2,1,0:T(8,128)(2,1)}, u32[]{:S(2)}, u32[]{:S(2)}) async-start(bf16[16,16,32,768]{3,2,1,0:T(8,128)(2,1)} %stack.3), calls=%async_computation.4 | async-start | bytes 25165824 | tf_op jit(solution)/shard_map/all_to_all | solution.py:91
  466.9 2.6 copy-start
  488.2 2.6 copy-start.3
Sparse Core Ops, SparseCore 0:
  162.7 273.7 all-gather.1
